TPU v7x, 32 devices: a whole 2x2x4 slice. The times are simulated.
32 devices in a mesh: grp: 2 (over y), seq: 4 (over x, core), head: 4 (over z).
Axes of the slice: x: 2, y: 2, z: 4, core: 2. Of those that a mesh axis runs over, the one named last changes fastest.
Arguments:
- activations: bfloat16 [16384, 2048], P(('grp', 'seq')), parts along dimension 0, may hold values from -6 to 6
- w_query: bfloat16 [2048, 2048], P(None, 'head'), may hold values from -0.125 to 0.125
- w_key: bfloat16 [2048, 2048], P(None, 'head'), may hold values from -0.125 to 0.125
- w_value: bfloat16 [2048, 2048], P(None, 'head'), may hold values from -0.125 to 0.125
- w_out: bfloat16 [2048, 2048], P('head', 'seq'), may hold values from -0.125 to 0.125
- log_decay: float32 [16, 16384], P('head', ('grp', 'seq')), parts along dimension 1, may hold values from -3 to 0, as said below
Outputs:
- mixed: bfloat16 [16384, 2048], P(('grp', 'seq', 'head')), parts along dimension 0
There are 2 independent parts, one for each index of `grp`. A program takes and returns all parts, laid end to end along the dimension named above; an argument that names none is the same for every part. Nothing has to cross between parts.
Inputs may be any that keep to these rules, and one draw needn't show every extreme that they name: `log_decay`: never positive.
All inputs are finite; a program needn't handle non-finite values.
Results may differ from a plain program's by a relative error of at most 0.0067.
Values may be sent and summed in bfloat16 or wider, within the bound.
No kernel may reach another device: no remote copies, remote signals or barrier semaphores. Data moves between devices by JAX's collectives and lax.ppermute only.
A program may use at most 128 MiB of HBM per device.

v0:
```python
import jax
import jax.numpy as jnp
from jax import lax
from jax.sharding import PartitionSpec as P

DH = 128
BLOCK = 256
HIGHEST = lax.Precision.HIGHEST


def carried_in(value, axis, join, neutral):
    count, mine = (lax.axis_size(axis), lax.axis_index(axis))
    pieces = jax.tree.map(lambda part: lax.all_gather(part, axis), value)
    subtotal = jax.tree.map(
        lambda part, zero: jnp.full_like(part, 0) + jnp.asarray(zero, part.dtype), value, neutral
    )

    def lap(position, subtotal):
        longer = join(subtotal, jax.tree.map(lambda part: part[position], pieces))
        return jax.tree.map(lambda new, old: jnp.where(position < mine, new, old), longer, subtotal)

    return lax.fori_loop(0, count - 1, lap, subtotal)


def combine_states(earlier, following):
    state_first, total_first = earlier
    state_second, total_second = following
    return (
        jnp.exp(total_second)[:, None, None] * state_first + state_second,
        total_first + total_second,
    )


def incoming(local_state, device_total):
    identity = (jnp.zeros_like(local_state), jnp.zeros_like(device_total))
    prefix_state, _ = carried_in((local_state, device_total), "seq", combine_states, identity)
    return prefix_state


def block_prefix(initial, updates, totals):

    def advance(carried, inputs_now):
        update_sum, block_total = inputs_now
        return (jnp.exp(block_total)[:, None, None] * carried + update_sum, carried)

    return lax.scan(advance, initial, (updates, totals.T))


def on_device(activations, w_query, w_key, w_value, w_out, log_decay):
    heads_here = log_decay.shape[0]
    tokens_here = activations.shape[0]
    blocks = tokens_here // BLOCK
    query = jnp.dot(activations, w_query, preferred_element_type=jnp.float32).astype(jnp.bfloat16)
    key_proj = jnp.dot(activations, w_key, preferred_element_type=jnp.float32).astype(jnp.bfloat16)
    value_proj = jnp.dot(activations, w_value, preferred_element_type=jnp.float32).astype(
        jnp.bfloat16
    )
    query_blocks = query.reshape(blocks, BLOCK, heads_here, DH)
    key_blocks = key_proj.reshape(blocks, BLOCK, heads_here, DH)
    query_wide = query_blocks.astype(jnp.float32)
    key_wide = key_blocks.astype(jnp.float32)
    value_wide = value_proj.astype(jnp.float32).reshape(blocks, BLOCK, heads_here, DH)
    within = jnp.cumsum(log_decay.reshape(heads_here, blocks, BLOCK), axis=2)
    totals = within[:, :, -1]
    causal = jnp.arange(BLOCK)[:, None] >= jnp.arange(BLOCK)[None, :]
    spread_log = within[:, :, :, None] - within[:, :, None, :]
    decay_mask = jnp.where(causal, jnp.exp(jnp.minimum(spread_log, 0.0)), 0.0)
    scores = jnp.einsum(
        "nthd,nshd->hnts", query_blocks, key_blocks, preferred_element_type=jnp.float32
    )
    within_block = jnp.einsum("hnts,nshd->nthd", scores * decay_mask, value_wide, precision=HIGHEST)
    carry_weight = jnp.exp(totals[:, :, None] - within)
    updates = jnp.einsum(
        "hns,nshd,nshe->nhde", carry_weight, key_wide, value_wide, precision=HIGHEST
    )
    device_total = jnp.sum(totals, axis=1)
    initial = jnp.zeros((heads_here, DH, DH), jnp.float32)
    local_state, before_blocks = block_prefix(initial, updates, totals)
    across_block = jnp.einsum(
        "hnt,nthd,nhde->nthe", jnp.exp(within), query_wide, before_blocks, precision=HIGHEST
    )
    prefix_state = incoming(local_state, device_total)
    earlier_sum = jnp.cumsum(totals, axis=1) - totals
    reach_weight = jnp.exp(within + earlier_sum[:, :, None])
    late_term = jnp.einsum(
        "hnt,nthd,hde->nthe", reach_weight, query_wide, prefix_state, precision=HIGHEST
    )
    attended = within_block + across_block + late_term
    attended = attended.reshape(tokens_here, heads_here, DH)
    normed = attended * lax.rsqrt(jnp.mean(attended * attended, axis=-1, keepdims=True) + 1e-05)
    normed = normed.astype(jnp.bfloat16).reshape(tokens_here, heads_here * DH)
    token_features = lax.all_to_all(normed, "head", split_axis=0, concat_axis=1, tiled=True)
    weight_rows = lax.all_gather(w_out, "head", axis=0, tiled=True)
    mixed = jnp.dot(
        token_features,
        lax.all_gather(weight_rows, "seq", axis=1, tiled=True),
        preferred_element_type=jnp.float32,
    )
    return mixed.astype(jnp.bfloat16)


def solution(mesh):
    return jax.shard_map(
        on_device,
        mesh=mesh,
        in_specs=(
            P(("grp", "seq"), None),
            P(None, "head"),
            P(None, "head"),
            P(None, "head"),
            P("head", "seq"),
            P("head", ("grp", "seq")),
        ),
        out_specs=P(("grp", "seq", "head"), None),
        check_vma=False,
    )
```

profile of v0, /device:TPU:0, one launch (start us, length us, event | category | flops | bytes accessed | tf_op | source)
XLA Modules:
  0.0 212.9 jit_solution(9722926669350448896)
XLA Ops:
  8.1 2.3 %reduce-window.6 = f32[4,8,2,128]{3,1,2,0:T(8,128)S(1)} reduce-window(f32[4,8,2,128]{3,1,2,0:T(8,128)S(1)} %copy.81, f32[]{:T(128)} %constant.50.clone.1), window={size=1x1x1x128 pad=0_0x0_0x0_0x127_0}, to_apply=%region_0.0 | reduce-window | flops 1040384 | bytes 65540 | tf_op jit(solution)/shard_map/reduce-window
  11.1 9.1 %convolution_convert_fusion.1 = bf16[2048,512]{1,0:T(8,128)(2,1)} fusion(bf16[2048,2048]{1,0:T(8,128)(2,1)} %param.10, bf16[2048,512]{1,0:T(8,128)(2,1)S(1)} %copy-done), kind=kOutput, calls=%fused_computation.30 | convolution fusion | flops 4296015872 | bytes 12582912 | tf_op jit(solution)/shard_map/dot_general | solution.py:54
  20.2 4.0 %reshape.92 = bf16[8,256,4,128]{3,2,1,0:T(4,128)(2,1)} reshape(bf16[2048,512]{1,0:T(8,128)(2,1)} %convolution_convert_fusion.1) | data formatting | bytes 4194304 | tf_op jit(solution)/shard_map/reshape | solution.py:59
  24.2 2.8 %copy.90 = bf16[8,256,4,128]{1,3,2,0:T(8,128)(2,1)S(1)} copy(bf16[8,256,4,128]{3,2,1,0:T(4,128)(2,1)} %reshape.92) | data formatting | bytes 4194304 | tf_op jit(solution)/shard_map/reshape | solution.py:59
  27.1 10.7 %convolution_convert_fusion.3 = bf16[2048,512]{1,0:T(8,128)(2,1)} fusion(bf16[2048,2048]{1,0:T(8,128)(2,1)} %param.10, bf16[2048,512]{1,0:T(8,128)(2,1)} %param.13), kind=kOutput, calls=%fused_computation.32 | convolution fusion | flops 4296015872 | bytes 12582912 | tf_op jit(solution)/shard_map/dot_general | solution.py:55
  37.7 4.0 %reshape.90 = bf16[8,256,4,128]{3,2,1,0:T(4,128)(2,1)} reshape(bf16[2048,512]{1,0:T(8,128)(2,1)} %convolution_convert_fusion.3) | data formatting | bytes 4194304 | tf_op jit(solution)/shard_map/reshape | solution.py:62
  41.8 5.4 %fusion.11 = f32[8,4,128,128]{3,2,1,0:T(8,128)} fusion(bf16[8,256,4,128]{1,3,2,0:T(8,128)(2,1)S(1)} %copy.90, f32[8,256,4]{1,2,0:T(4,128)S(1)} %copy.89, bf16[8,256,4,128]{3,2,1,0:T(4,128)(2,1)} %reshape.90), kind=kOutput, calls=%fused_computation.22 | convolution fusion | flops 1612709888 | bytes 6324224 | tf_op jit(solution)/shard_map/hns,nshd,nshe->nhde/dot_general | solution.py:73
  47.2 14.4 %while.27 = (s32[]{:T(128)}, f32[4,128,128]{2,1,0:T(8,128)S(1)}, f32[8,4,128,128]{3,2,1,0:T(8,128)}, f32[8,4]{1,0:T(8,128)S(1)}, f32[8,4,128,128]{3,2,1,0:T(8,128)}, /*index=5*/s32[]{:T(128)}, s32[]{:T(128)}) while((s32[]{:T(128)}, f32[4,128,128]{2,1,0:T(8,128)S(1)}, f32[8,4,128,128]{3,2,1,0:T(8,128)}, f32[8,4]{1,0:T(8,128)S(1)}, ...), condition=%wide.region_3.4_spmd.clone, body=%wide.region_2.3_spmd.clone.sunk | while | flops 262147 | bytes 1311376 | solution.py:46
  47.9 1.0 bitcast_add_fusion.5
  49.7 1.0 bitcast_add_fusion.5
  51.5 1.0 bitcast_add_fusion.5
  53.3 1.0 bitcast_add_fusion.5
  58.7 1.0 bitcast_add_fusion.5
  64.6 8.5 %all-reduce = f32[16]{0:T(128)S(1)} all-reduce(f32[16]{0:T(128)S(1)} %dynamic-update-slice), channel_id=2, replica_groups=mesh['grp'=2,'seq'=4,'head'=4] {'seq'}, use_global_device_ids=true, to_apply=%add | all-reduce | flops 16 | bytes 128
  73.2 9.2 %convolution_convert_fusion.2 = bf16[2048,512]{1,0:T(8,128)(2,1)} fusion(bf16[2048,2048]{1,0:T(8,128)(2,1)} %param.10, bf16[2048,512]{1,0:T(8,128)(2,1)S(1)} %copy-done.6), kind=kOutput, calls=%fused_computation.31 | convolution fusion | flops 4296015872 | bytes 12582912 | tf_op jit(solution)/shard_map/dot_general | solution.py:53
  82.4 2.5 %reshape.91 = bf16[8,256,4,128]{3,2,1,0:T(4,128)(2,1)S(1)} reshape(bf16[2048,512]{1,0:T(8,128)(2,1)} %convolution_convert_fusion.2) | data formatting | bytes 4194304 | tf_op jit(solution)/shard_map/reshape | solution.py:58
  85.0 7.9 %fusion.9 = f32[8,4,256,128]{2,3,1,0:T(8,128)} fusion(f32[8,4,128,128]{3,2,1,0:T(8,128)} %get-tuple-element.127, f32[8,256,4]{1,2,0:T(4,128)S(1)} %copy.87, bf16[8,256,4,128]{3,2,1,0:T(4,128)(2,1)S(1)} %reshape.91), kind=kOutput, calls=%fused_computation.16 | convolution fusion | flops 1612709888 | bytes 8421376 | tf_op jit(solution)/shard_map/hnt,nthd,nhde->nthe/dot_general | solution.py:79
  92.9 1.2 fusion.25
  94.7 8.8 %fusion.3 = f32[8,4,128,256]{3,2,1,0:T(8,128)} fusion(f32[4,8,256,256]{3,2,0,1:T(8,128)S(1)} %fusion.25, f32[4,8,256]{2,0,1:T(4,128)S(1)} %copy.84, pred[256,256]{1,0:T(8,128)(4,1)S(1)} %iota_compare_fusion, bf16[8,256,4,128]{3,2,1,0:T(4,128)(2,1)S(1)} %copy-done.5), kind=kOutput, calls=%fused_computation.8 | convolution fusion | flops 3229614080 | bytes 14778368 | tf_op jit(solution)/shard_map/hnts,nshd->nthd/dot_general | solution.py:71
  103.5 3.3 %while.28 = (s32[]{:T(128)}, f32[4,128,128]{2,1,0:T(8,128)S(1)}, s32[]{:T(128)}, f32[4,4]{1,0:T(4,128)S(1)}, f32[4,4,128,128]{3,2,1,0:T(8,128)}, /*index=5*/s32[]{:T(128)}, s32[]{:T(128)}) while((s32[]{:T(128)}, f32[4,128,128]{2,1,0:T(8,128)S(1)}, s32[]{:T(128)}, f32[4,4]{1,0:T(4,128)S(1)}, f32[4,4,128,128]{3,2,1,0:T(8,128)}, ...), condition=%wide.region_7.8_spmd.clone, body=%wide.region_6.7_spmd.clone.sunk | while | flops 262148 | bytes 786585 | solution.py:22
  103.5 1.1 fusion.44
  104.6 1.1 fusion.44
  105.7 1.1 fusion.44
  106.7 8.7 %multiply_reduce_fusion = (f32[8,256,4]{1,2,0:T(4,128)S(1)}, f32[8,256,4,128]{1,3,2,0:T(8,128)}) fusion(f32[4,128,128]{2,1,0:T(8,128)S(1)} %get-tuple-element.129, f32[8,256,4]{1,2,0:T(4,128)S(1)} %copy.94, bf16[8,256,4,128]{3,2,1,0:T(4,128)(2,1)S(1)} %reshape.91, f32[8,4,256,128]{2,3,1,0:T(8,128)} %fusion.9, f32[8,4,128,256]{3,2,1,0:T(8,128)} %fusion.3), kind=kOutput, calls=%fused_computation.21 | convolution fusion | flops 1616896000 | bytes 15007744 | tf_op jit(solution)/shard_map/hnt,nthd,hde->nthe/dot_general | solution.py:85
  115.9 3.9 %mul.51 = f32[2048,4,128]{2,1,0:T(4,128)} broadcast(f32[2048,4]{1,0:T(8,128)S(1)} %copy.97), dimensions={0,1} | broadcast | bytes 4227072 | tf_op jit(solution)/shard_map/mul | solution.py:90
  119.7 5.5 %mul.52 = f32[4,512,512]{2,1,0:T(8,128)} reshape(f32[2048,4,128]{2,1,0:T(4,128)} %mul.51) | data formatting | bytes 8388608 | tf_op jit(solution)/shard_map/mul | solution.py:90
  125.2 5.2 %copy.96 = f32[8,256,4,128]{3,2,1,0:T(4,128)} copy(f32[8,256,4,128]{1,3,2,0:T(8,128)} %get-tuple-element.219) | data formatting | bytes 8388608 | tf_op jit(solution)/shard_map/add | solution.py:88
  130.4 5.5 %reshape.95 = f32[4,512,512]{2,1,0:T(8,128)} reshape(f32[8,256,4,128]{3,2,1,0:T(4,128)} %copy.96) | data formatting | bytes 8388608 | tf_op jit(solution)/shard_map/reshape | solution.py:89
  135.9 4.2 %multiply_convert_fusion = bf16[4,512,512]{2,1,0:T(8,128)(2,1)S(1)} fusion(f32[4,512,512]{2,1,0:T(8,128)} %reshape.95, f32[4,512,512]{2,1,0:T(8,128)} %mul.52), kind=kLoop, calls=%fused_computation.20 | loop fusion | flops 2097152 | bytes 10485760 | tf_op jit(solution)/shard_map/convert_element_type | solution.py:91
  140.1 52.1 %all_to_all.16 = bf16[4,512,512]{2,1,0:T(8,128)(2,1)} all-to-all(bf16[4,512,512]{2,1,0:T(8,128)(2,1)S(1)} %multiply_convert_fusion), channel_id=1, replica_groups=mesh['grp'=2,'seq'=4,'head'=4] {'head'}, dimensions={0} | all-to-all | bytes 4194304 | tf_op jit(solution)/shard_map/all_to_all | solution.py:92
  192.2 4.2 %copy.98 = bf16[512,4,512]{0,2,1:T(8,128)(2,1)} copy(bf16[512,4,512]{2,0,1:T(8,128)(2,1)} %bitcast.63) | data formatting | bytes 4194304 | tf_op jit(solution)/shard_map/all_to_all | solution.py:92
  196.3 10.0 %convolution_convert_fusion = bf16[512,2048]{1,0:T(8,128)(2,1)} fusion(bf16[512,2048]{0,1:T(8,128)(2,1)} %bitcast.64, bf16[2048,2048]{1,0:T(8,128)(2,1)} %all-gather.8.cloned.1.call-done), kind=kOutput, calls=%fused_computation.29 | convolution fusion | flops 4296015872 | bytes 12582912 | tf_op jit(solution)/shard_map/dot_general | solution.py:94
  (74 shorter events, 14.7 us)
Async XLA Ops:
  6.5 4.6 %copy-start = (bf16[2048,512]{1,0:T(8,128)(2,1)S(1)}, bf16[2048,512]{1,0:T(8,128)(2,1)}, u32[]{:S(2)}) copy-start(bf16[2048,512]{1,0:T(8,128)(2,1)} %param.12) | copy-start | bytes 6291460
  6.5 55.9 %all-gather.6.cloned.1.call-start = ((), (), s32[]{:S(2)}) async-start(), calls=%async_computation.1 | async-start | bytes 2621440 | tf_op jit(solution)/shard_map/all_gather | solution.py:93
  7.3 96.2 %all-gather.10.cloned.1.call-start = ((), (), s32[]{:S(2)}) async-start(), calls=%async_computation.3 | async-start | bytes 1310720 | tf_op jit(solution)/shard_map/all_gather | solution.py:13
  27.1 14.7 %copy-start.3 = (bf16[8,256,4,128]{1,3,2,0:T(8,128)(2,1)}, bf16[8,256,4,128]{1,3,2,0:T(8,128)(2,1)S(1)}, u32[]{:S(2)}) copy-start(bf16[8,256,4,128]{1,3,2,0:T(8,128)(2,1)S(1)} %copy.90) | copy-start | bytes 6291460
  61.6 0.7 copy-start.2
  61.6 1.5 copy-start.7
  61.6 11.6 %copy-start.6 = (bf16[2048,512]{1,0:T(8,128)(2,1)S(1)}, bf16[2048,512]{1,0:T(8,128)(2,1)}, u32[]{:S(2)}) copy-start(bf16[2048,512]{1,0:T(8,128)(2,1)} %param.11) | copy-start | bytes 6291460
  62.3 134.0 %all-gather.8.cloned.1.call-start = ((), (), s32[]{:S(2)}) async-start(), calls=%async_computation.2 | async-start | bytes 10485760 | tf_op jit(solution)/shard_map/all_gather | solution.py:96
  85.0 7.9 %copy-start.4 = (bf16[8,256,4,128]{1,3,2,0:T(8,128)(2,1)S(1)}, bf16[8,256,4,128]{1,3,2,0:T(8,128)(2,1)}, u32[]{:S(2)}) copy-start(bf16[8,256,4,128]{1,3,2,0:T(8,128)(2,1)} %copy-done.3) | copy-start | bytes 6291460
  92.9 1.8 copy-start.5
  196.3 10.0 %copy-start.1 = (bf16[2048,512]{1,0:T(8,128)(2,1)S(1)}, bf16[2048,512]{1,0:T(8,128)(2,1)}, u32[]{:S(2)}) copy-start(bf16[2048,512]{1,0:T(8,128)(2,1)} %param.12) | copy-start | bytes 6291460
Sparse Core Ops, SparseCore 0:
  8.9 48.6 all-gather.5
  62.5 19.4 all-gather.9
  83.5 58.2 all-gather.7
where the time goes:
time: 214 us; the launch traced here: 213 us
  matrix products  71.1 us (33%)
  blocking collectives  60.5 us (28%)
  local copies, waits for them, and re-layouts  41.4 us (19%)
  other arithmetic  24.2 us (11%)
  between operations  14 us (7%)
    all_to_all x1, blocking collectives, on_device(): lax.all_to_all(normed, 'head', split_axis=0, concat_axis=1, tiled=True)  52.1 us
    dot_general x1, matrix products, on_device(): jnp.dot(activations, w_value, preferred_element_type=jnp.float32)  10.7 us
    dot_general x1, matrix products, on_device(): jnp.dot(token_features, lax.all_gather(weight_rows, 'seq', axis=1, tiled=...  10 us
    mul x2, local copies, waits for them, and re-layouts, on_device(): attended * lax.rsqrt(jnp.mean(attended * attended, axis=-1, keepdims=True...  9.33 us
    dot_general x1, matrix products, on_device(): jnp.dot(activations, w_query, preferred_element_type=jnp.float32)  9.19 us
    dot_general x1, matrix products, on_device(): jnp.dot(activations, w_key, preferred_element_type=jnp.float32)  9.11 us
    dot_general x1, matrix products, on_device(): jnp.einsum('hnts,nshd->nthd', scores * decay_mask, value_wide, precision=...  8.77 us
    dot_general x1, matrix products, on_device(): jnp.einsum('hnt,nthd,hde->nthe', reach_weight, query_wide, prefix_state,...  8.74 us
  transfers between devices with their start and end apart: 3, of which 0 were waited for; matrix products, arithmetic and copies ran while one was open for 59% of the time, Pallas kernels for 0%

commit v1 on v0

--- a/solution.py
+++ b/solution.py
@@ -89,7 +89,15 @@
     attended = attended.reshape(tokens_here, heads_here, DH)
     normed = attended * lax.rsqrt(jnp.mean(attended * attended, axis=-1, keepdims=True) + 1e-05)
     normed = normed.astype(jnp.bfloat16).reshape(tokens_here, heads_here * DH)
-    token_features = lax.all_to_all(normed, "head", split_axis=0, concat_axis=1, tiled=True)
+    token_features = jnp.concatenate(
+        jax.lax.all_to_all(
+            jnp.stack(jnp.split(normed, jax.lax.axis_size("head"), axis=0)),
+            "head",
+            split_axis=0,
+            concat_axis=0,
+        ),
+        axis=1,
+    )
     weight_rows = lax.all_gather(w_out, "head", axis=0, tiled=True)
     mixed = jnp.dot(
         token_features,

time: 214 us -> 202 us (0.944)
  local copies, waits for them, and re-layouts: 41.4 us -> 28.9 us
    mul x2 -> x0, local copies, waits for them, and re-layouts: 9.33 us -> none  [on_device(): attended * lax.rsqrt(jnp.mean(attended * attended, axis=-1, keepdims=True...]
    split x0 -> x5, local copies, waits for them, and re-layouts: none -> 6.65 us  [on_device(): jnp.split(normed, jax.lax.axis_size('head'), axis=0)]
    reshape x3 -> x2, local copies, waits for them, and re-layouts: 6.25 us -> 0.8 us  [the longest x1 5.45 us: on_device(): attended = attended.reshape(tokens_here, heads_here, DH)]
    all_to_all x1 -> x0, local copies, waits for them, and re-layouts: 4.18 us -> none  [on_device(): lax.all_to_all(normed, 'head', split_axis=0, concat_axis=1, tiled=True)]
  transfers between devices with their start and end apart: 3 -> 3, of which waited for: 0 -> 0; matrix products, arithmetic and copies ran while one was open for 59% -> 56% of each run, Pallas kernels for 0% -> 0%
where the time goes in v1:
time: 202 us; the launch traced here: 201 us
  matrix products  71 us (35%)
  blocking collectives  60.5 us (30%)
  local copies, waits for them, and re-layouts  28.9 us (14%)
  other arithmetic  24.8 us (12%)
  between operations  14 us (7%)
    all_to_all x1, blocking collectives, on_device(): jax.lax.all_to_all(jnp.stack(jnp.split(normed, jax.lax.axis_size('head'),...  52 us
    dot_general x1, matrix products, on_device(): jnp.dot(activations, w_value, preferred_element_type=jnp.float32)  10.6 us
    dot_general x1, matrix products, on_device(): jnp.dot(token_features, lax.all_gather(weight_rows, 'seq', axis=1, tiled=...  10 us
    dot_general x1, matrix products, on_device(): jnp.dot(activations, w_query, preferred_element_type=jnp.float32)  9.17 us
    dot_general x1, matrix products, on_device(): jnp.dot(activations, w_key, preferred_element_type=jnp.float32)  9.1 us
    dot_general x1, matrix products, on_device(): jnp.einsum('hnts,nshd->nthd', scores * decay_mask, value_wide, precision=...  8.76 us
    dot_general x1, matrix products, on_device(): jnp.einsum('hnt,nthd,hde->nthe', reach_weight, query_wide, prefix_state,...  8.73 us
    unnamed x1, blocking collectives  8.47 us
  transfers between devices with their start and end apart: 3, of which 0 were waited for; matrix products, arithmetic and copies ran while one was open for 56% of the time, Pallas kernels for 0%

profile of v1, /device:TPU:0, one launch (start us, length us, event | category | flops | bytes accessed | tf_op | source)
XLA Modules:
  0.0 200.9 jit_solution(5762278890452259732)
XLA Ops:
  8.1 2.3 %reduce-window.6 = f32[4,8,2,128]{3,1,2,0:T(8,128)S(1)} reduce-window(f32[4,8,2,128]{3,1,2,0:T(8,128)S(1)} %copy.62, f32[]{:T(128)} %constant.50.clone.1), window={size=1x1x1x128 pad=0_0x0_0x0_0x127_0}, to_apply=%region_0.0 | reduce-window | flops 1040384 | bytes 65540 | tf_op jit(solution)/shard_map/reduce-window
  11.1 9.1 %convolution_convert_fusion.1 = bf16[2048,512]{1,0:T(8,128)(2,1)} fusion(bf16[2048,2048]{1,0:T(8,128)(2,1)} %param.10, bf16[2048,512]{1,0:T(8,128)(2,1)S(1)} %copy-done), kind=kOutput, calls=%fused_computation.31 | convolution fusion | flops 4296015872 | bytes 12582912 | tf_op jit(solution)/shard_map/dot_general | solution.py:54
  20.2 4.0 %reshape.99 = bf16[8,256,4,128]{3,2,1,0:T(4,128)(2,1)} reshape(bf16[2048,512]{1,0:T(8,128)(2,1)} %convolution_convert_fusion.1) | data formatting | bytes 4194304 | tf_op jit(solution)/shard_map/reshape | solution.py:59
  24.2 2.8 %copy.71 = bf16[8,256,4,128]{1,3,2,0:T(8,128)(2,1)S(1)} copy(bf16[8,256,4,128]{3,2,1,0:T(4,128)(2,1)} %reshape.99) | data formatting | bytes 4194304 | tf_op jit(solution)/shard_map/reshape | solution.py:59
  27.0 10.6 %convolution_convert_fusion.3 = bf16[2048,512]{1,0:T(8,128)(2,1)} fusion(bf16[2048,2048]{1,0:T(8,128)(2,1)} %param.10, bf16[2048,512]{1,0:T(8,128)(2,1)} %param.13), kind=kOutput, calls=%fused_computation.33 | convolution fusion | flops 4296015872 | bytes 12582912 | tf_op jit(solution)/shard_map/dot_general | solution.py:55
  37.7 4.0 %reshape.97 = bf16[8,256,4,128]{3,2,1,0:T(4,128)(2,1)} reshape(bf16[2048,512]{1,0:T(8,128)(2,1)} %convolution_convert_fusion.3) | data formatting | bytes 4194304 | tf_op jit(solution)/shard_map/reshape | solution.py:62
  41.8 5.4 %fusion.12 = f32[8,4,128,128]{3,2,1,0:T(8,128)} fusion(bf16[8,256,4,128]{1,3,2,0:T(8,128)(2,1)S(1)} %copy.71, f32[8,256,4]{1,2,0:T(4,128)S(1)} %copy.70, bf16[8,256,4,128]{3,2,1,0:T(4,128)(2,1)} %reshape.97), kind=kOutput, calls=%fused_computation.23 | convolution fusion | flops 1612709888 | bytes 6324224 | tf_op jit(solution)/shard_map/hns,nshd,nshe->nhde/dot_general | solution.py:73
  47.2 14.4 %while.27 = (s32[]{:T(128)}, f32[4,128,128]{2,1,0:T(8,128)S(1)}, f32[8,4,128,128]{3,2,1,0:T(8,128)}, f32[8,4]{1,0:T(8,128)S(1)}, f32[8,4,128,128]{3,2,1,0:T(8,128)}, /*index=5*/s32[]{:T(128)}, s32[]{:T(128)}) while((s32[]{:T(128)}, f32[4,128,128]{2,1,0:T(8,128)S(1)}, f32[8,4,128,128]{3,2,1,0:T(8,128)}, f32[8,4]{1,0:T(8,128)S(1)}, ...), condition=%wide.region_3.4_spmd.clone, body=%wide.region_2.3_spmd.clone.sunk | while | flops 262147 | bytes 1311376 | solution.py:46
  47.9 1.0 bitcast_add_fusion.5
  49.7 1.0 bitcast_add_fusion.5
  51.5 1.0 bitcast_add_fusion.5
  53.3 1.0 bitcast_add_fusion.5
  64.6 8.5 %all-reduce = f32[16]{0:T(128)S(1)} all-reduce(f32[16]{0:T(128)S(1)} %dynamic-update-slice), channel_id=2, replica_groups=mesh['grp'=2,'seq'=4,'head'=4] {'seq'}, use_global_device_ids=true, to_apply=%add | all-reduce | flops 16 | bytes 128
  73.2 9.2 %convolution_convert_fusion.2 = bf16[2048,512]{1,0:T(8,128)(2,1)} fusion(bf16[2048,2048]{1,0:T(8,128)(2,1)} %param.10, bf16[2048,512]{1,0:T(8,128)(2,1)S(1)} %copy-done.7), kind=kOutput, calls=%fused_computation.32 | convolution fusion | flops 4296015872 | bytes 12582912 | tf_op jit(solution)/shard_map/dot_general | solution.py:53
  82.4 2.5 %reshape.98 = bf16[8,256,4,128]{3,2,1,0:T(4,128)(2,1)S(1)} reshape(bf16[2048,512]{1,0:T(8,128)(2,1)} %convolution_convert_fusion.2) | data formatting | bytes 4194304 | tf_op jit(solution)/shard_map/reshape | solution.py:58
  85.0 7.9 %fusion.9 = f32[8,4,256,128]{2,3,1,0:T(8,128)} fusion(f32[8,4,128,128]{3,2,1,0:T(8,128)} %get-tuple-element.127, f32[8,256,4]{1,2,0:T(4,128)S(1)} %copy.68, bf16[8,256,4,128]{3,2,1,0:T(4,128)(2,1)S(1)} %reshape.98), kind=kOutput, calls=%fused_computation.16 | convolution fusion | flops 1612709888 | bytes 8421376 | tf_op jit(solution)/shard_map/hnt,nthd,nhde->nthe/dot_general | solution.py:79
  92.9 1.2 fusion.26
  94.7 8.8 %fusion.3 = f32[8,4,128,256]{3,2,1,0:T(8,128)} fusion(f32[4,8,256,256]{3,2,0,1:T(8,128)S(1)} %fusion.26, f32[4,8,256]{2,0,1:T(4,128)S(1)} %copy.65, pred[256,256]{1,0:T(8,128)(4,1)S(1)} %iota_compare_fusion, bf16[8,256,4,128]{3,2,1,0:T(4,128)(2,1)S(1)} %copy-done.5), kind=kOutput, calls=%fused_computation.8 | convolution fusion | flops 3229614080 | bytes 14778368 | tf_op jit(solution)/shard_map/hnts,nshd->nthd/dot_general | solution.py:71
  103.5 3.3 %while.28 = (s32[]{:T(128)}, f32[4,128,128]{2,1,0:T(8,128)S(1)}, s32[]{:T(128)}, f32[4,4]{1,0:T(4,128)S(1)}, f32[4,4,128,128]{3,2,1,0:T(8,128)}, /*index=5*/s32[]{:T(128)}, s32[]{:T(128)}) while((s32[]{:T(128)}, f32[4,128,128]{2,1,0:T(8,128)S(1)}, s32[]{:T(128)}, f32[4,4]{1,0:T(4,128)S(1)}, f32[4,4,128,128]{3,2,1,0:T(8,128)}, ...), condition=%wide.region_7.8_spmd.clone, body=%wide.region_6.7_spmd.clone.sunk | while | flops 262148 | bytes 786585 | solution.py:22
  103.5 1.1 fusion.46
  104.6 1.1 fusion.46
  105.7 1.1 fusion.46
  106.8 8.7 %multiply_reduce_fusion = (f32[8,256,4]{1,2,0:T(4,128)S(1)}, f32[8,256,4,128]{1,3,2,0:T(8,128)}) fusion(f32[4,128,128]{2,1,0:T(8,128)S(1)} %get-tuple-element.129, f32[8,256,4]{1,2,0:T(4,128)S(1)} %copy.75, bf16[8,256,4,128]{3,2,1,0:T(4,128)(2,1)S(1)} %reshape.98, f32[8,4,256,128]{2,3,1,0:T(8,128)} %fusion.9, f32[8,4,128,256]{3,2,1,0:T(8,128)} %fusion.3), kind=kOutput, calls=%fused_computation.22 | convolution fusion | flops 1616896000 | bytes 15007744 | tf_op jit(solution)/shard_map/hnt,nthd,hde->nthe/dot_general | solution.py:85
  115.5 5.4 %copy.77 = f32[8,256,4,128]{3,1,0,2:T(8,128)} copy(f32[8,256,4,128]{1,3,2,0:T(8,128)} %get-tuple-element.218) | data formatting | bytes 8388608 | tf_op jit(solution)/shard_map/add | solution.py:88
  120.9 3.1 %fusion.11 = bf16[2048,4,128]{2,0,1:T(8,128)(2,1)S(1)} fusion(f32[8,256,4,128]{3,1,0,2:T(8,128)} %copy.77, f32[2048,4]{0,1:T(4,128)S(1)} %bitcast.78), kind=kLoop, calls=%fused_computation.19 | loop fusion | flops 2097152 | bytes 6324224 | tf_op jit(solution)/shard_map/convert_element_type | solution.py:91
  124.0 1.2 fusion.32
  125.2 1.3 copy.78
  126.5 2.1 %copy.79 = bf16[512,4,128]{0,2,1:T(8,128)(2,1)} copy(bf16[512,4,128]{2,0,1:T(8,128)(2,1)} %get-tuple-element.214) | data formatting | bytes 1048576 | tf_op jit(solution)/shard_map/split | solution.py:94
  128.6 1.1 copy.80
  130.6 1.6 pad_maximum_fusion
  132.3 52.0 %all_to_all.5 = bf16[4,512,512]{1,2,0:T(8,128)(2,1)} all-to-all(bf16[4,512,512]{1,2,0:T(8,128)(2,1)S(1)} %pad_maximum_fusion), channel_id=1, replica_groups=mesh['grp'=2,'seq'=4,'head'=4] {'head'}, dimensions={0} | all-to-all | bytes 4194304 | tf_op jit(solution)/shard_map/all_to_all | solution.py:93
  184.3 10.0 %convolution_convert_fusion = bf16[512,2048]{1,0:T(8,128)(2,1)} fusion(bf16[512,2048]{0,1:T(8,128)(2,1)} %bitcast.72, bf16[2048,2048]{1,0:T(8,128)(2,1)} %all-gather.8.cloned.1.call-done), kind=kOutput, calls=%fused_computation.30 | convolution fusion | flops 4296015872 | bytes 12582912 | tf_op jit(solution)/shard_map/dot_general | solution.py:102
  (77 shorter events, 16.5 us)
Async XLA Ops:
  6.5 4.6 %copy-start = (bf16[2048,512]{1,0:T(8,128)(2,1)S(1)}, bf16[2048,512]{1,0:T(8,128)(2,1)}, u32[]{:S(2)}) copy-start(bf16[2048,512]{1,0:T(8,128)(2,1)} %param.12) | copy-start | bytes 6291460
  6.5 55.8 %all-gather.6.cloned.1.call-start = ((), (), s32[]{:S(2)}) async-start(), calls=%async_computation.1 | async-start | bytes 2621440 | tf_op jit(solution)/shard_map/all_gather | solution.py:101
  7.3 96.2 %all-gather.10.cloned.1.call-start = ((), (), s32[]{:S(2)}) async-start(), calls=%async_computation.3 | async-start | bytes 1310720 | tf_op jit(solution)/shard_map/all_gather | solution.py:13
  27.0 14.7 %copy-start.3 = (bf16[8,256,4,128]{1,3,2,0:T(8,128)(2,1)}, bf16[8,256,4,128]{1,3,2,0:T(8,128)(2,1)S(1)}, u32[]{:S(2)}) copy-start(bf16[8,256,4,128]{1,3,2,0:T(8,128)(2,1)S(1)} %copy.71) | copy-start | bytes 6291460
  61.6 0.7 copy-start.2
  61.6 1.5 copy-start.8
  61.6 11.6 %copy-start.7 = (bf16[2048,512]{1,0:T(8,128)(2,1)S(1)}, bf16[2048,512]{1,0:T(8,128)(2,1)}, u32[]{:S(2)}) copy-start(bf16[2048,512]{1,0:T(8,128)(2,1)} %param.11) | copy-start | bytes 6291460
  62.3 122.0 %all-gather.8.cloned.1.call-start = ((), (), s32[]{:S(2)}) async-start(), calls=%async_computation.2 | async-start | bytes 10485760 | tf_op jit(solution)/shard_map/all_gather | solution.py:104
  85.0 7.9 %copy-start.4 = (bf16[8,256,4,128]{1,3,2,0:T(8,128)(2,1)S(1)}, bf16[8,256,4,128]{1,3,2,0:T(8,128)(2,1)}, u32[]{:S(2)}) copy-start(bf16[8,256,4,128]{1,3,2,0:T(8,128)(2,1)} %copy-done.3) | copy-start | bytes 6291460
  92.9 1.8 copy-start.5
  125.2 3.4 %copy-start.6 = (bf16[512,4,128]{2,0,1:T(8,128)(2,1)S(1)}, bf16[512,4,128]{2,0,1:T(8,128)(2,1)}, u32[]{:S(2)}) copy-start(bf16[512,4,128]{2,0,1:T(8,128)(2,1)} %get-tuple-element.213) | copy-start | bytes 1572868
  184.3 10.0 %copy-start.1 = (bf16[2048,512]{1,0:T(8,128)(2,1)S(1)}, bf16[2048,512]{1,0:T(8,128)(2,1)}, u32[]{:S(2)}) copy-start(bf16[2048,512]{1,0:T(8,128)(2,1)} %param.12) | copy-start | bytes 6291460
Sparse Core Ops, SparseCore 0:
  8.9 48.6 all-gather.5
  62.4 19.4 all-gather.9
  83.5 58.2 all-gather.7
